TPU v7x, 128 devices: a whole 4x4x4 slice. The times are simulated.
128 devices in a mesh: row: 8 (over z, core), col: 16 (over x, y).
Axes of the slice: x: 4, y: 4, z: 4, core: 2. Of those that a mesh axis runs over, the one named last changes fastest.
Arguments:
- nodes: bfloat16 [65536, 512], P(('row', 'col')), may hold values from -6 to 6
- cotangent: bfloat16 [65536, 512], P(('row', 'col')), may hold values from -6 to 6
- edge_source: int32 [262144], P(('row', 'col')), may hold values from 0 to 639
- edge_target: int32 [262144], P(('row', 'col')), may hold values from 0 to 511
- halo_lists: int32 [128, 4, 32], P(('row', 'col')), may hold values from 0 to 511
- pool_owner: int32 [65536], P(('row', 'col')), may hold values from 0 to 127, as said below
- pool_table: int32 [128, 1024], P(('row', 'col')), may hold values from -1 to 127, as said below
- source_weight: bfloat16 [512, 512], replicated, may hold values from -0.25 to 0.25
- target_weight: bfloat16 [512, 512], replicated, may hold values from -0.25 to 0.25
- edge_weight: bfloat16 [512, 512], replicated, may hold values from -0.25 to 0.25
- inner_weight: bfloat16 [1024, 512], replicated, may hold values from -0.1875 to 0.1875
- outer_weight: bfloat16 [512, 512], replicated, may hold values from -0.25 to 0.25
- coarse_weight: bfloat16 [512, 512], replicated, may hold values from -0.5 to 0.5
Outputs:
- updated: bfloat16 [65536, 512], P(('row', 'col'))
- node_gradient: float32 [65536, 512], P(('row', 'col'))
- source_gradient: float32 [512, 512], replicated
- target_gradient: float32 [512, 512], replicated
- edge_gradient: float32 [512, 512], replicated
- inner_gradient: float32 [1024, 512], replicated
- outer_gradient: float32 [512, 512], replicated
- coarse_gradient: float32 [512, 512], replicated
Inputs may be any that keep to these rules, and one draw needn't show every extreme that they name: `edge_source`: rows below 512 are the partition's own nodes; row 512 + k * 32 + j is row j of halo block k. `pool_owner`: at most 8 nodes of one partition name the same owner; one owner is named by exactly 8 nodes of every partition. `pool_table`: entry [o, q * 8 + k] is the coarse row of owner o for the node of rank k among the nodes of partition q that name o, and -1 where q names o fewer than k + 1 times.
All inputs are finite; a program needn't handle non-finite values.
Results may differ from a plain program's by a relative error of at most 0.014.
Values may be sent and summed in bfloat16 or wider, within the bound.
No kernel may reach another device: no remote copies, remote signals or barrier semaphores. Data moves between devices by JAX's collectives and lax.ppermute only.
A program may use at most 128 MiB of HBM per device.

v0:
```python
import math
import jax
import jax.numpy as jnp
from jax import lax
from jax.sharding import PartitionSpec as P


def passed_along(value, axis, steps):
    count = lax.axis_size(axis)
    initial, last = (max(0, -steps), min(count, count - steps))
    return lax.ppermute(value, axis, [(source, source + steps) for source in range(initial, last)])


def product(first, second):
    return jnp.dot(first, second, preferred_element_type=jnp.float32)


def left_product(first, second):
    return lax.dot_general(
        first, second, (((0,), (0,)), ((), ())), preferred_element_type=jnp.float32
    )


def right_product(first, second):
    return lax.dot_general(
        first, second, (((1,), (1,)), ((), ())), preferred_element_type=jnp.float32
    )


def silu_slope(value):
    sigma = jax.nn.sigmoid(value)
    return sigma * (1.0 + value * (1.0 - sigma))


def trade_halo(blocks, flip):
    moved = []
    for number, offset in enumerate((1, -1)):
        moved.append(passed_along(blocks[number], "row", offset * flip))
    for number, offset in enumerate((1, -1)):
        moved.append(passed_along(blocks[2 + number], "col", offset * flip))
    return moved


def trade_slots(buffer):
    return lax.all_to_all(buffer, ("row", "col"), split_axis=0, concat_axis=0, tiled=True)


def toward_owners(values, slot, devices, capacity, trader):
    width = values.shape[1]
    outgoing = jnp.zeros((devices * capacity, width), values.dtype).at[slot].set(values)
    arrived = trader(outgoing.reshape(devices, capacity, width))
    return arrived.reshape(devices * capacity, width)


def toward_sources(coarse_values, table, slot, devices, capacity, trader):
    width = coarse_values.shape[1]
    picked = jnp.take(coarse_values, jnp.maximum(table, 0), axis=0)
    picked = jnp.where((table >= 0)[:, None], picked, jnp.zeros_like(picked))
    returned = trader(picked.reshape(devices, capacity, width)).reshape(devices * capacity, width)
    return jnp.take(returned, slot, axis=0)


def local(
    nodes,
    cotangent,
    edge_source,
    edge_target,
    halo_lists,
    pool_owner,
    pool_table,
    source_weight,
    target_weight,
    edge_weight,
    inner_weight,
    outer_weight,
    coarse_weight,
):
    devices = lax.axis_size("row") * lax.axis_size("col")
    count_rows, width = nodes.shape
    lists = halo_lists[0]
    halo_rows = lists.shape[1]
    table = pool_table[0]
    capacity = table.shape[0] // devices
    coarse_rows = count_rows // 4
    scale = 1.0 / math.sqrt(count_rows * devices)
    received = trade_halo([jnp.take(nodes, lists[number], axis=0) for number in range(4)], 1)
    extended = jnp.concatenate([nodes] + received, axis=0)
    source_side = product(extended, source_weight)
    target_side = product(nodes, target_weight)
    edge_linear = jnp.take(source_side, edge_source, axis=0) + jnp.take(
        target_side, edge_target, axis=0
    )
    edge_hidden = jax.nn.silu(edge_linear).astype(jnp.bfloat16)
    message_linear = product(edge_hidden, edge_weight)
    aggregate = jax.ops.segment_sum(jax.nn.silu(message_linear), edge_target, count_rows).astype(
        jnp.bfloat16
    )
    joined = jnp.concatenate([nodes, aggregate], axis=1)
    node_linear = product(joined, inner_weight)
    node_hidden = jax.nn.silu(node_linear).astype(jnp.bfloat16)
    refined = (nodes.astype(jnp.float32) + product(node_hidden, outer_weight)).astype(jnp.bfloat16)
    owner_hot = (pool_owner[:, None] == jnp.arange(devices, dtype=jnp.int32)[None, :]).astype(
        jnp.bfloat16
    )
    positions = jnp.arange(count_rows, dtype=jnp.int32)
    lower = (positions[:, None] > positions[None, :]).astype(jnp.bfloat16)
    rank = jnp.sum(product(lower, owner_hot) * owner_hot, axis=1).astype(jnp.int32)
    slot = pool_owner * capacity + rank
    member = (jnp.arange(coarse_rows, dtype=jnp.int32)[:, None] == table[None, :]).astype(
        jnp.bfloat16
    )
    count = jnp.maximum(jnp.sum(member, axis=1, dtype=jnp.float32), 1.0)[:, None]
    arrived = toward_owners(refined, slot, devices, capacity, trade_slots)
    coarse = (product(member, arrived) / count).astype(jnp.bfloat16)
    coarse_linear = product(coarse, coarse_weight)
    coarse_update = jax.nn.silu(coarse_linear).astype(jnp.bfloat16)
    parent_rows = toward_sources(coarse_update, table, slot, devices, capacity, trade_slots)
    arrived_grad = toward_owners(cotangent, slot, devices, capacity, trade_slots)
    grad_coarse = (product(member, arrived_grad) * silu_slope(coarse_linear)).astype(jnp.bfloat16)
    coarse_share = (right_product(grad_coarse, coarse_weight) / count).astype(jnp.bfloat16)
    share_rows = toward_sources(coarse_share, table, slot, devices, capacity, trade_slots)
    updated = (refined.astype(jnp.float32) + parent_rows.astype(jnp.float32)).astype(jnp.bfloat16)
    coarse_gradient = left_product(coarse, grad_coarse)
    grad_refined = cotangent.astype(jnp.float32) + share_rows.astype(jnp.float32)
    refined_low = grad_refined.astype(jnp.bfloat16)
    outer_gradient = left_product(node_hidden, refined_low)
    grad_hidden = (right_product(refined_low, outer_weight) * silu_slope(node_linear)).astype(
        jnp.bfloat16
    )
    inner_gradient = left_product(joined, grad_hidden)
    grad_joined = right_product(grad_hidden, inner_weight)
    grad_aggregate = grad_joined[:, width:].astype(jnp.bfloat16)
    grad_message = (
        jnp.take(grad_aggregate, edge_target, axis=0) * silu_slope(message_linear)
    ).astype(jnp.bfloat16)
    edge_gradient = left_product(edge_hidden, grad_message)
    grad_edges = right_product(grad_message, edge_weight) * silu_slope(edge_linear)
    grad_sources = jax.ops.segment_sum(grad_edges, edge_source, extended.shape[0]).astype(
        jnp.bfloat16
    )
    grad_targets = jax.ops.segment_sum(grad_edges, edge_target, count_rows).astype(jnp.bfloat16)
    source_gradient = left_product(extended, grad_sources)
    target_gradient = left_product(nodes, grad_targets)
    (
        source_gradient,
        target_gradient,
        edge_gradient,
        inner_gradient,
        outer_gradient,
        coarse_gradient,
    ) = lax.psum(
        (
            source_gradient,
            target_gradient,
            edge_gradient,
            inner_gradient,
            outer_gradient,
            coarse_gradient,
        ),
        ("row", "col"),
    )
    grad_extended = right_product(grad_sources, source_weight)
    back_blocks = grad_extended[count_rows:].astype(jnp.bfloat16).reshape(4, halo_rows, width)
    returned = trade_halo([back_blocks[number] for number in range(4)], -1)
    node_gradient = (
        grad_refined
        + grad_joined[:, :width]
        + right_product(grad_targets, target_weight)
        + grad_extended[:count_rows]
    )
    node_gradient = node_gradient.at[lists.reshape(-1)].add(
        jnp.concatenate(returned, axis=0).astype(jnp.float32)
    )
    return (
        updated,
        node_gradient,
        source_gradient * scale,
        target_gradient * scale,
        edge_gradient * scale,
        inner_gradient * scale,
        outer_gradient * scale,
        coarse_gradient * scale,
    )


def solution(mesh):
    in_specs = (
        P(("row", "col"), None),
        P(("row", "col"), None),
        P(("row", "col")),
        P(("row", "col")),
        P(("row", "col"), None, None),
        P(("row", "col")),
        P(("row", "col"), None),
        P(),
        P(),
        P(),
        P(),
        P(),
        P(),
    )
    out_specs = (P(("row", "col"), None), P(("row", "col"), None), P(), P(), P(), P(), P(), P())
    return jax.shard_map(local, mesh=mesh, in_specs=in_specs, out_specs=out_specs, check_vma=False)
```

profile of v0, /device:TPU:1, one launch (start us, length us, event | category | flops | bytes accessed | tf_op | source)
XLA Modules:
  0.0 423.6 jit_solution(16720933355326291041)
XLA Ops:
  8.1 1.7 gather_fusion.3
  9.9 4.9 %collective-permute-start = (bf16[32,512]{1,0:T(8,128)(2,1)S(1)}, bf16[32,512]{1,0:T(8,128)(2,1)S(1)}, u32[]{:S(2)}, u32[]{:S(2)}) collective-permute-start(bf16[32,512]{1,0:T(8,128)(2,1)S(1)} %broadcast_select_fusion.4), channel_id=1, source_target_pairs={{0,16},{16,32},{32,48},{48,64},{64,80},{80,96},{96,112},{1,17},{17... | collective-permute-start | bytes 98312 | tf_op jit(solution)/shard_map/ppermute | solution.py:11
  14.8 1.7 gather_fusion.4
  16.7 1.9 collective-permute-start.1
  18.6 1.7 gather_fusion.5
  20.4 3.2 collective-permute-start.2
  23.6 1.7 gather_fusion.6
  28.8 1.6 fusion.57
  32.1 8.9 %gather_fusion.1 = f32[2048,512]{1,0:T(8,128)} fusion(f32[512,512]{1,0:T(8,128)S(1)} %fusion.57, s32[2048]{0:T(1024)S(1)} %get-tuple-element.46), kind=kCustom, calls=%fused_computation.9 | custom fusion | bytes 8396800 | tf_op jit(solution)/shard_map/jit(_take)/gather | solution.py:90
  42.6 8.9 %gather_fusion = f32[2048,512]{1,0:T(8,128)} fusion(f32[640,512]{1,0:T(8,128)S(1)} %fusion.56, s32[2048]{0:T(1024)S(1)} %get-tuple-element.45), kind=kCustom, calls=%fused_computation.8 | custom fusion | bytes 8396800 | tf_op jit(solution)/shard_map/jit(_take)/gather | solution.py:90
  51.6 4.2 %multiply_convert_fusion.1 = bf16[2048,512]{1,0:T(8,128)(2,1)S(1)} fusion(f32[2048,512]{1,0:T(8,128)} %gather_fusion.1, pred[2048]{0:T(1024)(128)(4,1)} %get-tuple-element.47, f32[2048,512]{1,0:T(8,128)} %gather_fusion, pred[2048]{0:T(1024)(128)(4,1)} %get-tuple-element.48), kind=kLoop, calls=%fused_computation.22 | loop fusion | flops 8388608 | bytes 10489856 | tf_op jit(solution)/shard_map/convert_element_type | solution.py:93
  57.1 3.3 fusion.58
  60.4 14.6 %scatter_custom_fusion = f32[512,512]{1,0:T(8,128)S(1)} fusion(s32[2048]{0:T(1024)} %param.22, f32[2048,512]{1,0:T(8,128)} %fusion.58, f32[]{:T(128)} %constant.62.clone.1, f32[]{:T(128)} %constant.52.clone.1), kind=kCustom, calls=%fused_computation.19 | custom fusion | flops 5242880 | bytes 5243904 | tf_op jit(solution)/shard_map/scatter-add | solution.py:95
  77.2 3.6 scatter_custom_fusion.1
  80.8 11.6 %all-to-all-start = ((bf16[128,8,512]{2,1,0:T(8,128)(2,1)}), bf16[128,8,512]{2,1,0:T(8,128)(2,1)S(1)}, u32[]{:S(2)}, u32[]{:S(2)}) async-start(bf16[128,8,512]{2,1,0:T(8,128)(2,1)} %bitcast.5), calls=%async_computation | async-start | bytes 2097152 | tf_op jit(solution)/shard_map/all_to_all | solution.py:45
  92.4 4.0 scatter_custom_fusion.2
  96.4 14.7 %all-to-all-done = bf16[128,8,512]{2,1,0:T(8,128)(2,1)S(1)} async-done(((bf16[128,8,512]{2,1,0:T(8,128)(2,1)}), bf16[128,8,512]{2,1,0:T(8,128)(2,1)S(1)}, u32[]{:S(2)}, u32[]{:S(2)}) %all-to-all-start) | async-done | bytes 1048608 | tf_op jit(solution)/shard_map/all_to_all | solution.py:45
  111.2 5.7 %all-to-all-start.2 = ((bf16[128,8,512]{2,1,0:T(8,128)(2,1)}), bf16[128,8,512]{2,1,0:T(8,128)(2,1)}, u32[]{:S(2)}, u32[]{:S(2)}) async-start(bf16[128,8,512]{2,1,0:T(8,128)(2,1)} %bitcast.9), calls=%async_computation.2 | async-start | bytes 2097152 | tf_op jit(solution)/shard_map/all_to_all | solution.py:45
  119.2 16.3 %all-to-all-done.2 = bf16[128,8,512]{2,1,0:T(8,128)(2,1)} async-done(((bf16[128,8,512]{2,1,0:T(8,128)(2,1)}), bf16[128,8,512]{2,1,0:T(8,128)(2,1)}, u32[]{:S(2)}, u32[]{:S(2)}) %all-to-all-start.2) | async-done | bytes 1048608 | tf_op jit(solution)/shard_map/all_to_all | solution.py:45
  139.1 4.0 gather_fusion.9
  143.1 5.1 %gather_fusion.7 = bf16[1024,512]{1,0:T(8,128)(2,1)} fusion(bf16[128,512]{1,0:T(8,128)(2,1)S(1)} %get-tuple-element.41, s32[1024]{0:T(1024)S(1)} %maximum_clamp_fusion), kind=kCustom, calls=%fused_computation.1.clone | custom fusion | bytes 2101248 | tf_op jit(solution)/shard_map/jit(_take)/gather | solution.py:57
  148.2 2.9 fusion.12
  151.1 4.8 %all-to-all-start.3 = ((bf16[128,8,512]{2,1,0:T(8,128)(2,1)}), bf16[128,8,512]{2,1,0:T(8,128)(2,1)S(1)}, u32[]{:S(2)}, u32[]{:S(2)}) async-start(bf16[128,8,512]{2,1,0:T(8,128)(2,1)} %get-tuple-element.33), calls=%async_computation.3 | async-start | bytes 2097152 | tf_op jit(solution)/shard_map/all_to_all | solution.py:45
  156.0 2.3 fusion.61
  158.3 16.6 %all-to-all-done.3 = bf16[128,8,512]{2,1,0:T(8,128)(2,1)S(1)} async-done(((bf16[128,8,512]{2,1,0:T(8,128)(2,1)}), bf16[128,8,512]{2,1,0:T(8,128)(2,1)S(1)}, u32[]{:S(2)}, u32[]{:S(2)}) %all-to-all-start.3) | async-done | bytes 1048608 | tf_op jit(solution)/shard_map/all_to_all | solution.py:45
  174.9 2.6 gather_fusion.10
  177.5 2.4 fusion.5
  182.1 9.2 %gather_fusion.2 = bf16[2048,512]{1,0:T(8,128)(2,1)} fusion(bf16[512,512]{1,0:T(8,128)(2,1)S(1)} %slice.97, s32[2048]{0:T(1024)S(1)} %get-tuple-element.46), kind=kCustom, calls=%fused_computation.10 | custom fusion | bytes 4202496 | tf_op jit(solution)/shard_map/jit(_take)/gather | solution.py:134
  191.3 3.8 multiply_convert_fusion
  197.4 4.3 %multiply_multiply_fusion = f32[2048,512]{1,0:T(8,128)} fusion(bf16[2048,512]{1,0:T(8,128)(2,1)S(1)} %multiply_convert_fusion, bf16[512,512]{1,0:T(8,128)(2,1)S(1)} %copy-done.20, f32[2048,512]{1,0:T(8,128)S(1)} %copy-done.2, pred[2048]{0:T(1024)(128)(4,1)S(1)} %copy-done.31, f32[2048,512]{1,0:T(8,128)S(1)} %copy-done.3, pred[2048]{0:T(1024)(128)(4,1)S(1)} %copy-done.32), kind=kOutput, calls=%fused_computation.17 | convolution fusion | flops 1085276160 | bytes 15208448 | tf_op jit(solution)/shard_map/dot_general | solution.py:25
  201.6 13.6 %scatter_custom_fusion.4 = f32[640,512]{1,0:T(8,128)S(1)} fusion(s32[2048]{0:T(1024)} %param.21, f32[2048,512]{1,0:T(8,128)} %multiply_multiply_fusion, f32[]{:T(128)} %constant.52.clone.1), kind=kCustom, calls=%fused_computation.59 | custom fusion | flops 1048576 | bytes 1311232 | tf_op jit(solution)/shard_map/scatter-add | solution.py:138
  215.2 13.7 %scatter_custom_fusion.3 = f32[512,512]{1,0:T(8,128)S(1)} fusion(s32[2048]{0:T(1024)} %param.22, f32[2048,512]{1,0:T(8,128)} %multiply_multiply_fusion, f32[]{:T(128)} %constant.52.clone.1), kind=kCustom, calls=%fused_computation.73 | custom fusion | flops 1048576 | bytes 1049088 | tf_op jit(solution)/shard_map/scatter-add | solution.py:141
  229.0 4.9 %fusion.60 = f32[512,512]{1,0:T(8,128)} fusion(bf16[2048,512]{1,0:T(8,128)(2,1)} %copy-done.5, bf16[2048,512]{1,0:T(8,128)(2,1)} %copy-done.10), kind=kOutput, calls=%fused_computation.144 | convolution fusion | flops 1073741824 | bytes 5242880 | tf_op jit(solution)/shard_map/dot_general | solution.py:19
  233.9 2.1 fusion.15
  236.0 1.7 fusion.51
  237.6 1.6 fusion.27
  240.7 4.7 %all-to-all-start.1 = ((bf16[128,8,512]{2,1,0:T(8,128)(2,1)}), bf16[128,8,512]{2,1,0:T(8,128)(2,1)S(1)}, u32[]{:S(2)}, u32[]{:S(2)}) async-start(bf16[128,8,512]{2,1,0:T(8,128)(2,1)} %get-tuple-element.34), calls=%async_computation.1 | async-start | bytes 2097152 | tf_op jit(solution)/shard_map/all_to_all | solution.py:45
  245.5 22.7 %all-to-all-done.1 = bf16[128,8,512]{2,1,0:T(8,128)(2,1)S(1)} async-done(((bf16[128,8,512]{2,1,0:T(8,128)(2,1)}), bf16[128,8,512]{2,1,0:T(8,128)(2,1)S(1)}, u32[]{:S(2)}, u32[]{:S(2)}) %all-to-all-start.1) | async-done | bytes 1048608 | tf_op jit(solution)/shard_map/all_to_all | solution.py:45
  268.2 2.0 gather_fusion.8
  270.3 1.7 fusion.55
  272.0 2.4 collective-permute-start.7
  275.7 3.1 collective-permute-start.5
  278.8 1.9 collective-permute-start.4
  280.8 1.6 fusion.3
  284.1 1.8 scatter_custom_fusion.5
  285.9 121.3 %all-reduce.3.cloned.1.call-done = (f32[512,512]{1,0:T(8,128)}, f32[512,512]{1,0:T(8,128)}, f32[512,512]{1,0:T(8,128)}, f32[1024,512]{1,0:T(8,128)}, f32[512,512]{1,0:T(8,128)}, /*index=5*/f32[512,512]{1,0:T(8,128)}) async-done(((f32[512,512]{1,0:T(8,128)}, f32[512,512]{1,0:T(8,128)}, f32[512,512]{1,0:T(8,128)}, f32[1024,512]{1,0:T(8,128)}, f32[512,512]{1,0:T(8,128)}, /*index=5*/f32[512,512]{1,0:T(8,128)}), ...) | async-done | bytes 7340048 | tf_op jit(solution)/shard_map/psum | solution.py:151
  407.2 2.4 broadcast_multiply_fusion.5
  409.6 2.4 broadcast_multiply_fusion.4
  (142 shorter events, 31.0 us)
Async XLA Ops:
  7.2 68.0 %copy-start = (bf16[1024,512]{1,0:T(8,128)(2,1)S(1)}, bf16[1024,512]{1,0:T(8,128)(2,1)}, u32[]{:S(2)}) copy-start(bf16[1024,512]{1,0:T(8,128)(2,1)} %param.29) | copy-start | bytes 3145732
  7.2 24.9 %copy-start.4 = (bf16[512,512]{1,0:T(8,128)(2,1)S(1)}, bf16[512,512]{1,0:T(8,128)(2,1)}, u32[]{:S(2)}) copy-start(bf16[512,512]{1,0:T(8,128)(2,1)} %param.19) | copy-start | bytes 1572868
  7.2 24.3 %copy-start.39 = (s32[512]{0:T(512)S(1)}, s32[512]{0:T(512)}, u32[]{:S(2)}) copy-start(s32[512]{0:T(512)} %param.24) | copy-start | bytes 6148
  9.9 31.1 %collective-permute-start = (bf16[32,512]{1,0:T(8,128)(2,1)S(1)}, bf16[32,512]{1,0:T(8,128)(2,1)S(1)}, u32[]{:S(2)}, u32[]{:S(2)}) collective-permute-start(bf16[32,512]{1,0:T(8,128)(2,1)S(1)} %broadcast_select_fusion.4), channel_id=1, source_target_pairs={{0,16},{16,32},{32,48},{48,64},{64,80},{80,96},{96,112},{1,17},{17... | collective-permute-start | bytes 98312 | tf_op jit(solution)/shard_map/ppermute | solution.py:11
  16.7 24.4 %collective-permute-start.1 = (bf16[32,512]{1,0:T(8,128)(2,1)S(1)}, bf16[32,512]{1,0:T(8,128)(2,1)S(1)}, u32[]{:S(2)}, u32[]{:S(2)}) collective-permute-start(bf16[32,512]{1,0:T(8,128)(2,1)S(1)} %broadcast_select_fusion.3), channel_id=1, source_target_pairs={{16,0},{32,16},{48,32},{64,48},{80,64},{96,80},{112,96},{17,1},{33... | collective-permute-start | bytes 98312 | tf_op jit(solution)/shard_map/ppermute | solution.py:11
  20.4 20.6 %collective-permute-start.2 = (bf16[32,512]{1,0:T(8,128)(2,1)S(1)}, bf16[32,512]{1,0:T(8,128)(2,1)S(1)}, u32[]{:S(2)}, u32[]{:S(2)}) collective-permute-start(bf16[32,512]{1,0:T(8,128)(2,1)S(1)} %broadcast_select_fusion.2), channel_id=1, source_target_pairs={{0,1},{1,2},{2,3},{3,4},{4,5},{5,6},{6,7},{7,8},{8,9},{9,10},{10,1... | collective-permute-start | bytes 98312 | tf_op jit(solution)/shard_map/ppermute | solution.py:11
  25.5 15.6 %collective-permute-start.3 = (bf16[32,512]{1,0:T(8,128)(2,1)S(1)}, bf16[32,512]{1,0:T(8,128)(2,1)S(1)}, u32[]{:S(2)}, u32[]{:S(2)}) collective-permute-start(bf16[32,512]{1,0:T(8,128)(2,1)S(1)} %broadcast_select_fusion.1), channel_id=1, source_target_pairs={{1,0},{2,1},{3,2},{4,3},{5,4},{6,5},{7,6},{8,7},{9,8},{10,9},{11,1... | collective-permute-start | bytes 98312 | tf_op jit(solution)/shard_map/ppermute | solution.py:11
  51.6 5.5 %copy-start.19 = (bf16[512,512]{1,0:T(8,128)(2,1)S(1)}, bf16[512,512]{1,0:T(8,128)(2,1)}, u32[]{:S(2)}) copy-start(bf16[512,512]{1,0:T(8,128)(2,1)} %param.28) | copy-start | bytes 1572868
  76.2 20.1 %copy-start.30 = (s32[1,1024]{1,0:T(1,128)S(1)}, s32[1,1024]{1,0:T(1,128)}, u32[]{:S(2)}) copy-start(s32[1,1024]{1,0:T(1,128)} %param.25) | copy-start | bytes 12292
  80.8 30.4 %all-to-all-start = ((bf16[128,8,512]{2,1,0:T(8,128)(2,1)}), bf16[128,8,512]{2,1,0:T(8,128)(2,1)S(1)}, u32[]{:S(2)}, u32[]{:S(2)}) async-start(bf16[128,8,512]{2,1,0:T(8,128)(2,1)} %bitcast.5), calls=%async_computation | async-start | bytes 2097152 | tf_op jit(solution)/shard_map/all_to_all | solution.py:45
  111.2 24.4 %all-to-all-start.2 = ((bf16[128,8,512]{2,1,0:T(8,128)(2,1)}), bf16[128,8,512]{2,1,0:T(8,128)(2,1)}, u32[]{:S(2)}, u32[]{:S(2)}) async-start(bf16[128,8,512]{2,1,0:T(8,128)(2,1)} %bitcast.9), calls=%async_computation.2 | async-start | bytes 2097152 | tf_op jit(solution)/shard_map/all_to_all | solution.py:45
  116.9 18.6 %copy-start.41 = (f32[128]{0:T(128)}, f32[128]{0:T(128)S(1)}, u32[]{:S(2)}) copy-start(f32[128]{0:T(128)S(1)} %broadcast_maximum_fusion) | copy-start | bytes 1540
  117.8 19.2 %copy-start.28 = (bf16[128,512]{1,0:T(8,128)(2,1)}, bf16[128,512]{1,0:T(8,128)(2,1)S(1)}, u32[]{:S(2)}) copy-start(bf16[128,512]{1,0:T(8,128)(2,1)S(1)} %fusion.7) | copy-start | bytes 393220
  143.1 5.1 %copy-start.37 = (pred[1024]{0:T(1024)(128)(4,1)S(1)}, pred[1024]{0:T(1024)(128)(4,1)}, u32[]{:S(2)}) copy-start(pred[1024]{0:T(1024)(128)(4,1)} %get-tuple-element.31) | copy-start | bytes 3076
  143.1 5.1 %copy-start.38 = (pred[1024]{0:T(1024)(128)(4,1)S(1)}, pred[1024]{0:T(1024)(128)(4,1)}, u32[]{:S(2)}) copy-start(pred[1024]{0:T(1024)(128)(4,1)} %get-tuple-element.32) | copy-start | bytes 3076
  148.2 7.8 %copy-start.34 = (s32[512]{0:T(512)S(1)}, s32[512]{0:T(512)}, u32[]{:S(2)}) copy-start(s32[512]{0:T(512)} %get-tuple-element.18) | copy-start | bytes 6148
  151.1 26.4 %copy-start.35 = (pred[512]{0:T(512)(128)(4,1)S(1)}, pred[512]{0:T(512)(128)(4,1)}, u32[]{:S(2)}) copy-start(pred[512]{0:T(512)(128)(4,1)} %get-tuple-element.17) | copy-start | bytes 1540
  151.1 23.8 %all-to-all-start.3 = ((bf16[128,8,512]{2,1,0:T(8,128)(2,1)}), bf16[128,8,512]{2,1,0:T(8,128)(2,1)S(1)}, u32[]{:S(2)}, u32[]{:S(2)}) async-start(bf16[128,8,512]{2,1,0:T(8,128)(2,1)} %get-tuple-element.33), calls=%async_computation.3 | async-start | bytes 2097152 | tf_op jit(solution)/shard_map/all_to_all | solution.py:45
  155.9 251.3 %all-reduce.3.cloned.1.call-start = ((), (), s32[]{:S(2)}) async-start(), calls=%async_computation.4 | async-start | bytes 14680064 | tf_op jit(solution)/shard_map/psum | solution.py:151
  182.1 9.2 %copy-start.31 = (pred[2048]{0:T(1024)(128)(4,1)S(1)}, pred[2048]{0:T(1024)(128)(4,1)}, u32[]{:S(2)}) copy-start(pred[2048]{0:T(1024)(128)(4,1)} %get-tuple-element.47) | copy-start | bytes 6148
  182.1 14.4 %copy-start.20 = (bf16[512,512]{1,0:T(8,128)(2,1)S(1)}, bf16[512,512]{1,0:T(8,128)(2,1)}, u32[]{:S(2)}) copy-start(bf16[512,512]{1,0:T(8,128)(2,1)} %param.28) | copy-start | bytes 1572868
  191.3 5.1 %copy-start.2 = (f32[2048,512]{1,0:T(8,128)S(1)}, f32[2048,512]{1,0:T(8,128)}, u32[]{:S(2)}) copy-start(f32[2048,512]{1,0:T(8,128)} %gather_fusion.1) | copy-start | bytes 12582916
  191.3 6.1 %copy-start.3 = (f32[2048,512]{1,0:T(8,128)S(1)}, f32[2048,512]{1,0:T(8,128)}, u32[]{:S(2)}) copy-start(f32[2048,512]{1,0:T(8,128)} %gather_fusion) | copy-start | bytes 12582916
  191.3 6.1 %copy-start.32 = (pred[2048]{0:T(1024)(128)(4,1)S(1)}, pred[2048]{0:T(1024)(128)(4,1)}, u32[]{:S(2)}) copy-start(pred[2048]{0:T(1024)(128)(4,1)} %get-tuple-element.48) | copy-start | bytes 6148
  228.9 10.3 %copy-start.6 = (f32[512,512]{1,0:T(8,128)}, f32[512,512]{1,0:T(8,128)S(1)}, u32[]{:S(2)}) copy-start(f32[512,512]{1,0:T(8,128)S(1)} %scatter_custom_fusion.3) | copy-start | bytes 3145732
  228.9 4.9 %copy-start.23 = (bf16[512,512]{1,0:T(8,128)(2,1)S(1)}, bf16[512,512]{1,0:T(8,128)(2,1)}, u32[]{:S(2)}) copy-start(bf16[512,512]{1,0:T(8,128)(2,1)} %copy-done.22) | copy-start | bytes 1572868
  228.9 4.9 %copy-start.25 = (bf16[512,512]{1,0:T(8,128)(2,1)S(1)}, bf16[512,512]{1,0:T(8,128)(2,1)}, u32[]{:S(2)}) copy-start(bf16[512,512]{1,0:T(8,128)(2,1)} %copy-done.24) | copy-start | bytes 1572868
  229.0 7.0 %copy-start.11 = (bf16[512,512]{1,0:T(8,128)(2,1)S(1)}, bf16[512,512]{1,0:T(8,128)(2,1)}, u32[]{:S(2)}) copy-start(bf16[512,512]{1,0:T(8,128)(2,1)} %gather_fusion.10) | copy-start | bytes 1572868
  229.0 7.0 %copy-start.21 = (bf16[512,512]{1,0:T(8,128)(2,1)S(1)}, bf16[512,512]{1,0:T(8,128)(2,1)}, u32[]{:S(2)}) copy-start(bf16[512,512]{1,0:T(8,128)(2,1)} %param.20) | copy-start | bytes 1572868
  229.0 7.0 %copy-start.36 = (pred[512]{0:T(512)(128)(4,1)S(1)}, pred[512]{0:T(512)(128)(4,1)}, u32[]{:S(2)}) copy-start(pred[512]{0:T(512)(128)(4,1)} %get-tuple-element.17) | copy-start | bytes 1540
  229.0 7.0 %copy-start.43 = (f32[512,512]{1,0:T(8,128)S(1)}, f32[512,512]{1,0:T(8,128)}, u32[]{:S(2)}) copy-start(f32[512,512]{1,0:T(8,128)} %copy-done.42) | copy-start | bytes 3145732
  240.7 4.7 %copy-start.33 = (s32[1,4,32]{2,1,0:T(4,128)S(1)}, s32[1,4,32]{2,1,0:T(4,128)}, u32[]{:S(2)}) copy-start(s32[1,4,32]{2,1,0:T(4,128)} %param.23) | copy-start | bytes 1540
  240.7 27.5 %all-to-all-start.1 = ((bf16[128,8,512]{2,1,0:T(8,128)(2,1)}), bf16[128,8,512]{2,1,0:T(8,128)(2,1)S(1)}, u32[]{:S(2)}, u32[]{:S(2)}) async-start(bf16[128,8,512]{2,1,0:T(8,128)(2,1)} %get-tuple-element.34), calls=%async_computation.1 | async-start | bytes 2097152 | tf_op jit(solution)/shard_map/all_to_all | solution.py:45
  268.2 12.5 %copy-start.12 = (bf16[512,512]{1,0:T(8,128)(2,1)S(1)}, bf16[512,512]{1,0:T(8,128)(2,1)}, u32[]{:S(2)}) copy-start(bf16[512,512]{1,0:T(8,128)(2,1)} %gather_fusion.10) | copy-start | bytes 1572868
  270.2 10.6 %copy-start.7 = (f32[512,512]{1,0:T(8,128)S(1)}, f32[512,512]{1,0:T(8,128)}, u32[]{:S(2)}) copy-start(f32[512,512]{1,0:T(8,128)} %copy-done.6) | copy-start | bytes 3145732
  270.2 10.6 %copy-start.9 = (f32[512,1024]{1,0:T(8,128)S(1)}, f32[512,1024]{1,0:T(8,128)}, u32[]{:S(2)}) copy-start(f32[512,1024]{1,0:T(8,128)} %copy-done.8) | copy-start | bytes 6291460
  270.2 10.6 %copy-start.14 = (bf16[512,512]{1,0:T(8,128)(2,1)S(1)}, bf16[512,512]{1,0:T(8,128)(2,1)}, u32[]{:S(2)}) copy-start(bf16[512,512]{1,0:T(8,128)(2,1)} %param.27) | copy-start | bytes 1572868
  270.2 12.2 %copy-start.27 = (bf16[512,512]{1,0:T(8,128)(2,1)S(1)}, bf16[512,512]{1,0:T(8,128)(2,1)}, u32[]{:S(2)}) copy-start(bf16[512,512]{1,0:T(8,128)(2,1)} %copy-done.26) | copy-start | bytes 1572868
  272.0 11.5 %collective-permute-start.7 = (bf16[32,512]{1,0:T(8,128)(2,1)S(1)}, bf16[32,512]{1,0:T(8,128)(2,1)S(1)}, u32[]{:S(2)}, u32[]{:S(2)}) collective-permute-start(bf16[32,512]{1,0:T(8,128)(2,1)S(1)} %get-tuple-element.28), channel_id=1, source_target_pairs={{0,1},{1,2},{2,3},{3,4},{4,5},{5,6},{6,7},{7,8},{8,9},{9,10},{10,1... | collective-permute-start | bytes 98312 | tf_op jit(solution)/shard_map/ppermute | solution.py:11
  274.4 9.1 %collective-permute-start.6 = (bf16[32,512]{1,0:T(8,128)(2,1)S(1)}, bf16[32,512]{1,0:T(8,128)(2,1)S(1)}, u32[]{:S(2)}, u32[]{:S(2)}) collective-permute-start(bf16[32,512]{1,0:T(8,128)(2,1)S(1)} %get-tuple-element.29), channel_id=1, source_target_pairs={{1,0},{2,1},{3,2},{4,3},{5,4},{6,5},{7,6},{8,7},{9,8},{10,9},{11,1... | collective-permute-start | bytes 98312 | tf_op jit(solution)/shard_map/ppermute | solution.py:11
  275.7 7.8 %collective-permute-start.5 = (bf16[32,512]{1,0:T(8,128)(2,1)S(1)}, bf16[32,512]{1,0:T(8,128)(2,1)S(1)}, u32[]{:S(2)}, u32[]{:S(2)}) collective-permute-start(bf16[32,512]{1,0:T(8,128)(2,1)S(1)} %get-tuple-element.30), channel_id=1, source_target_pairs={{0,16},{16,32},{32,48},{48,64},{64,80},{80,96},{96,112},{1,17},{17... | collective-permute-start | bytes 98312 | tf_op jit(solution)/shard_map/ppermute | solution.py:11
  278.8 5.2 %collective-permute-start.4 = (bf16[32,512]{1,0:T(8,128)(2,1)S(1)}, bf16[32,512]{1,0:T(8,128)(2,1)S(1)}, u32[]{:S(2)}, u32[]{:S(2)}) collective-permute-start(bf16[32,512]{1,0:T(8,128)(2,1)S(1)} %get-tuple-element.27), channel_id=1, source_target_pairs={{16,0},{32,16},{48,32},{64,48},{80,64},{96,80},{112,96},{17,1},{33... | collective-permute-start | bytes 98312 | tf_op jit(solution)/shard_map/ppermute | solution.py:11
  285.8 128.8 %copy-start.18 = (f32[512,512]{1,0:T(8,128)}, f32[512,512]{1,0:T(8,128)S(1)}, u32[]{:S(2)}) copy-start(f32[512,512]{1,0:T(8,128)S(1)} %scatter_custom_fusion.5) | copy-start | bytes 3145732
  407.2 4.8 %copy-start.17 = (f32[512,512]{1,0:T(8,128)S(1)}, f32[512,512]{1,0:T(8,128)}, u32[]{:S(2)}) copy-start(f32[512,512]{1,0:T(8,128)} %get-tuple-element.13) | copy-start | bytes 3145732
  407.2 5.9 %copy-start.13 = (f32[1024,512]{1,0:T(8,128)S(1)}, f32[1024,512]{1,0:T(8,128)}, u32[]{:S(2)}) copy-start(f32[1024,512]{1,0:T(8,128)} %get-tuple-element.14) | copy-start | bytes 6291460
  409.6 5.0 %copy-start.16 = (f32[512,512]{1,0:T(8,128)S(1)}, f32[512,512]{1,0:T(8,128)}, u32[]{:S(2)}) copy-start(f32[512,512]{1,0:T(8,128)} %get-tuple-element.15) | copy-start | bytes 3145732
  412.0 3.7 copy-start.15
  413.1 3.7 copy-start.1
  (9 other events, 12.6 us)
Sparse Core Ops, SparseCore 0:
  240.8 166.3 all-reduce.2
where the time goes:
time: 425 us; the launch traced here: 424 us
  waiting for transfers between devices  192 us (45%)
  other arithmetic  69.8 us (16%)
  local copies, waits for them, and re-layouts  62 us (15%)
  starting transfers between devices  46.9 us (11%)
  matrix products  38 us (9%)
  between operations  14.8 us (3%)
    psum x1, waiting for transfers between devices, local(): lax.psum((source_gradient, target_gradient, edge_gradient, inner_gradient...  121 us
    all_to_all x4, waiting for transfers between devices, trade_slots(): lax.all_to_all(buffer, ('row', 'col'), split_axis=0, concat_axis=0, tiled...  70.4 us
    all_to_all x4, starting transfers between devices, trade_slots(): lax.all_to_all(buffer, ('row', 'col'), split_axis=0, concat_axis=0, tiled...  26.8 us
    ppermute x8, starting transfers between devices, passed_along(): lax.ppermute(value, axis, [(source, source + steps) for source in range(i...  20 us
    scatter-add x1, other arithmetic, local(): jax.ops.segment_sum(jax.nn.silu(message_linear), edge_target, count_rows)  14.6 us
    dot_general x6, matrix products, left_product(): lax.dot_general(first, second, (((0,), (0,)), ((), ())), preferred_elemen...  13.9 us
    scatter-add x1, other arithmetic, local(): jax.ops.segment_sum(grad_edges, edge_target, count_rows)  13.7 us
    scatter-add x1, other arithmetic, local(): jax.ops.segment_sum(grad_edges, edge_source, extended.shape[0])  13.6 us
  transfers between devices with their start and end apart: 13, of which 6 were waited for; matrix products, arithmetic and copies ran while one was open for 9% of the time, Pallas kernels for 0%

commit v1 on v0

--- a/solution.py
+++ b/solution.py
@@ -149,15 +149,18 @@
         outer_gradient,
         coarse_gradient,
     ) = lax.psum(
-        (
-            source_gradient,
-            target_gradient,
-            edge_gradient,
-            inner_gradient,
-            outer_gradient,
-            coarse_gradient,
+        lax.psum(
+            (
+                source_gradient,
+                target_gradient,
+                edge_gradient,
+                inner_gradient,
+                outer_gradient,
+                coarse_gradient,
+            ),
+            "row",
         ),
-        ("row", "col"),
+        "col",
     )
     grad_extended = right_product(grad_sources, source_weight)
     back_blocks = grad_extended[count_rows:].astype(jnp.bfloat16).reshape(4, halo_rows, width)

time: 425 us -> 493 us (1.16)
  waiting for transfers between devices: 192 us -> 256 us
    psum x0 -> x1, waiting for transfers between devices: none -> 90.3 us  [local(): lax.psum(lax.psum((source_gradient, target_gradient, edge_gradient, inner...]
    psum x1, waiting for transfers between devices: 121 us -> 90.1 us  [local(): lax.psum((source_gradient, target_gradient, edge_gradient, inner_gradient...]
  transfers between devices with their start and end apart: 13 -> 14, of which waited for: 6 -> 7; matrix products, arithmetic and copies ran while one was open for 9% -> 7% of each run, Pallas kernels for 0% -> 0%
where the time goes in v1:
time: 493 us; the launch traced here: 491 us
  waiting for transfers between devices  256 us (52%)
  other arithmetic  69.7 us (14%)
  local copies, waits for them, and re-layouts  62 us (13%)
  starting transfers between devices  51.3 us (10%)
  matrix products  38 us (8%)
  between operations  14.8 us (3%)
    psum x1, waiting for transfers between devices, local(): lax.psum(lax.psum((source_gradient, target_gradient, edge_gradient, inner...  90.3 us
    psum x1, waiting for transfers between devices, local(): lax.psum((source_gradient, target_gradient, edge_gradient, inner_gradient...  90.1 us
    all_to_all x4, waiting for transfers between devices, trade_slots(): lax.all_to_all(buffer, ('row', 'col'), split_axis=0, concat_axis=0, tiled...  74.1 us
    all_to_all x4, starting transfers between devices, trade_slots(): lax.all_to_all(buffer, ('row', 'col'), split_axis=0, concat_axis=0, tiled...  30.5 us
    ppermute x8, starting transfers between devices, passed_along(): lax.ppermute(value, axis, [(source, source + steps) for source in range(i...  20.7 us
    scatter-add x1, other arithmetic, local(): jax.ops.segment_sum(jax.nn.silu(message_linear), edge_target, count_rows)  14.6 us
    dot_general x6, matrix products, left_product(): lax.dot_general(first, second, (((0,), (0,)), ((), ())), preferred_elemen...  13.9 us
    scatter-add x1, other arithmetic, local(): jax.ops.segment_sum(grad_edges, edge_target, count_rows)  13.7 us
  transfers between devices with their start and end apart: 14, of which 7 were waited for; matrix products, arithmetic and copies ran while one was open for 7% of the time, Pallas kernels for 0%

profile of v1, /device:TPU:1, one launch (start us, length us, event | category | flops | bytes accessed | tf_op | source)
XLA Modules:
  0.0 491.3 jit_solution(2963278642442166886)
XLA Ops:
  8.1 1.7 gather_fusion.3
  9.9 4.9 %collective-permute-start = (bf16[32,512]{1,0:T(8,128)(2,1)S(1)}, bf16[32,512]{1,0:T(8,128)(2,1)S(1)}, u32[]{:S(2)}, u32[]{:S(2)}) collective-permute-start(bf16[32,512]{1,0:T(8,128)(2,1)S(1)} %broadcast_select_fusion.4), channel_id=1, source_target_pairs={{0,16},{16,32},{32,48},{48,64},{64,80},{80,96},{96,112},{1,17},{17... | collective-permute-start | bytes 98312 | tf_op jit(solution)/shard_map/ppermute | solution.py:11
  14.8 1.7 gather_fusion.4
  16.7 1.9 collective-permute-start.1
  18.6 1.7 gather_fusion.5
  20.4 3.2 collective-permute-start.2
  23.6 1.7 gather_fusion.6
  28.8 1.6 fusion.57
  32.1 8.9 %gather_fusion.1 = f32[2048,512]{1,0:T(8,128)} fusion(f32[512,512]{1,0:T(8,128)S(1)} %fusion.57, s32[2048]{0:T(1024)S(1)} %get-tuple-element.52), kind=kCustom, calls=%fused_computation.9 | custom fusion | bytes 8396800 | tf_op jit(solution)/shard_map/jit(_take)/gather | solution.py:90
  42.6 9.0 %gather_fusion = f32[2048,512]{1,0:T(8,128)} fusion(f32[640,512]{1,0:T(8,128)S(1)} %fusion.56, s32[2048]{0:T(1024)S(1)} %get-tuple-element.51), kind=kCustom, calls=%fused_computation.8 | custom fusion | bytes 8396800 | tf_op jit(solution)/shard_map/jit(_take)/gather | solution.py:90
  51.6 4.2 multiply_convert_fusion.1
  57.1 3.3 fusion.58
  60.5 14.6 %scatter_custom_fusion = f32[512,512]{1,0:T(8,128)S(1)} fusion(s32[2048]{0:T(1024)} %param.22, f32[2048,512]{1,0:T(8,128)} %fusion.58, f32[]{:T(128)} %constant.62.clone.1, f32[]{:T(128)} %constant.52.clone.1), kind=kCustom, calls=%fused_computation.19 | custom fusion | flops 5242880 | bytes 5243904 | tf_op jit(solution)/shard_map/scatter-add | solution.py:95
  77.2 3.6 scatter_custom_fusion.1
  80.8 11.6 %all-to-all-start = ((bf16[128,8,512]{2,1,0:T(8,128)(2,1)}), bf16[128,8,512]{2,1,0:T(8,128)(2,1)S(1)}, u32[]{:S(2)}, u32[]{:S(2)}) async-start(bf16[128,8,512]{2,1,0:T(8,128)(2,1)} %bitcast.5), calls=%async_computation | async-start | bytes 2097152 | tf_op jit(solution)/shard_map/all_to_all | solution.py:45
  92.4 4.0 scatter_custom_fusion.2
  96.5 14.7 %all-to-all-done = bf16[128,8,512]{2,1,0:T(8,128)(2,1)S(1)} async-done(((bf16[128,8,512]{2,1,0:T(8,128)(2,1)}), bf16[128,8,512]{2,1,0:T(8,128)(2,1)S(1)}, u32[]{:S(2)}, u32[]{:S(2)}) %all-to-all-start) | async-done | bytes 1048608 | tf_op jit(solution)/shard_map/all_to_all | solution.py:45
  111.2 5.7 %all-to-all-start.2 = ((bf16[128,8,512]{2,1,0:T(8,128)(2,1)}), bf16[128,8,512]{2,1,0:T(8,128)(2,1)}, u32[]{:S(2)}, u32[]{:S(2)}) async-start(bf16[128,8,512]{2,1,0:T(8,128)(2,1)} %bitcast.9), calls=%async_computation.2 | async-start | bytes 2097152 | tf_op jit(solution)/shard_map/all_to_all | solution.py:45
  119.2 16.3 %all-to-all-done.2 = bf16[128,8,512]{2,1,0:T(8,128)(2,1)} async-done(((bf16[128,8,512]{2,1,0:T(8,128)(2,1)}), bf16[128,8,512]{2,1,0:T(8,128)(2,1)}, u32[]{:S(2)}, u32[]{:S(2)}) %all-to-all-start.2) | async-done | bytes 1048608 | tf_op jit(solution)/shard_map/all_to_all | solution.py:45
  139.1 4.0 gather_fusion.9
  143.1 5.1 %gather_fusion.7 = bf16[1024,512]{1,0:T(8,128)(2,1)} fusion(bf16[128,512]{1,0:T(8,128)(2,1)S(1)} %get-tuple-element.47, s32[1024]{0:T(1024)S(1)} %maximum_clamp_fusion), kind=kCustom, calls=%fused_computation.1.clone | custom fusion | bytes 2101248 | tf_op jit(solution)/shard_map/jit(_take)/gather | solution.py:57
  148.2 2.9 fusion.12
  151.1 4.8 all-to-all-start.3
  156.0 2.3 fusion.61
  158.3 16.6 %all-to-all-done.3 = bf16[128,8,512]{2,1,0:T(8,128)(2,1)S(1)} async-done(((bf16[128,8,512]{2,1,0:T(8,128)(2,1)}), bf16[128,8,512]{2,1,0:T(8,128)(2,1)S(1)}, u32[]{:S(2)}, u32[]{:S(2)}) %all-to-all-start.3) | async-done | bytes 1048608 | tf_op jit(solution)/shard_map/all_to_all | solution.py:45
  174.9 2.6 gather_fusion.10
  177.5 2.4 fusion.5
  182.1 9.2 %gather_fusion.2 = bf16[2048,512]{1,0:T(8,128)(2,1)} fusion(bf16[512,512]{1,0:T(8,128)(2,1)S(1)} %slice.97, s32[2048]{0:T(1024)S(1)} %get-tuple-element.52), kind=kCustom, calls=%fused_computation.10 | custom fusion | bytes 4202496 | tf_op jit(solution)/shard_map/jit(_take)/gather | solution.py:134
  191.3 3.8 multiply_convert_fusion
  197.4 4.3 multiply_multiply_fusion
  201.7 13.6 %scatter_custom_fusion.4 = f32[640,512]{1,0:T(8,128)S(1)} fusion(s32[2048]{0:T(1024)} %param.21, f32[2048,512]{1,0:T(8,128)} %multiply_multiply_fusion, f32[]{:T(128)} %constant.52.clone.1), kind=kCustom, calls=%fused_computation.59 | custom fusion | flops 1048576 | bytes 1311232 | tf_op jit(solution)/shard_map/scatter-add | solution.py:138
  215.2 13.7 %scatter_custom_fusion.3 = f32[512,512]{1,0:T(8,128)S(1)} fusion(s32[2048]{0:T(1024)} %param.22, f32[2048,512]{1,0:T(8,128)} %multiply_multiply_fusion, f32[]{:T(128)} %constant.52.clone.1), kind=kCustom, calls=%fused_computation.73 | custom fusion | flops 1048576 | bytes 1049088 | tf_op jit(solution)/shard_map/scatter-add | solution.py:141
  229.0 4.9 fusion.60
  233.9 2.1 fusion.15
  236.0 1.7 fusion.51
  240.8 90.1 %all-reduce.7.cloned.1.call-done = (f32[512,512]{1,0:T(8,128)}, f32[512,512]{1,0:T(8,128)}, f32[512,512]{1,0:T(8,128)}, f32[1024,512]{1,0:T(8,128)}, f32[512,512]{1,0:T(8,128)}, /*index=5*/f32[512,512]{1,0:T(8,128)}) async-done(((f32[512,512]{1,0:T(8,128)}, f32[512,512]{1,0:T(8,128)}, f32[512,512]{1,0:T(8,128)}, f32[1024,512]{1,0:T(8,128)}, f32[512,512]{1,0:T(8,128)}, /*index=5*/f32[512,512]{1,0:T(8,128)}), ...) | async-done | bytes 7340048 | tf_op jit(solution)/shard_map/psum | solution.py:152
  330.9 8.4 %all-to-all-start.1 = ((bf16[128,8,512]{2,1,0:T(8,128)(2,1)}), bf16[128,8,512]{2,1,0:T(8,128)(2,1)S(1)}, u32[]{:S(2)}, u32[]{:S(2)}) async-start(bf16[128,8,512]{2,1,0:T(8,128)(2,1)} %get-tuple-element.40), calls=%async_computation.1 | async-start | bytes 2097152 | tf_op jit(solution)/shard_map/all_to_all | solution.py:45
  339.4 26.4 %all-to-all-done.1 = bf16[128,8,512]{2,1,0:T(8,128)(2,1)S(1)} async-done(((bf16[128,8,512]{2,1,0:T(8,128)(2,1)}), bf16[128,8,512]{2,1,0:T(8,128)(2,1)S(1)}, u32[]{:S(2)}, u32[]{:S(2)}) %all-to-all-start.1) | async-done | bytes 1048608 | tf_op jit(solution)/shard_map/all_to_all | solution.py:45
  365.9 2.0 gather_fusion.8
  367.9 1.7 fusion.55
  369.7 2.3 collective-permute-start.7
  373.3 3.8 collective-permute-start.5
  377.1 1.9 collective-permute-start.4
  379.1 1.7 fusion.3
  382.8 1.8 scatter_custom_fusion.5
  384.6 90.3 %all-reduce.5.cloned.1.call-done = (f32[512,512]{1,0:T(8,128)}, f32[512,512]{1,0:T(8,128)}, f32[512,512]{1,0:T(8,128)}, f32[1024,512]{1,0:T(8,128)}, f32[512,512]{1,0:T(8,128)}, /*index=5*/f32[512,512]{1,0:T(8,128)}) async-done(((f32[512,512]{1,0:T(8,128)}, f32[512,512]{1,0:T(8,128)}, f32[512,512]{1,0:T(8,128)}, f32[1024,512]{1,0:T(8,128)}, f32[512,512]{1,0:T(8,128)}, /*index=5*/f32[512,512]{1,0:T(8,128)}), ...) | async-done | bytes 7340048 | tf_op jit(solution)/shard_map/psum | solution.py:151
  474.8 2.4 broadcast_multiply_fusion.5
  477.3 2.4 broadcast_multiply_fusion.4
  (145 shorter events, 32.9 us)
Async XLA Ops:
  7.2 68.0 %copy-start = (bf16[1024,512]{1,0:T(8,128)(2,1)S(1)}, bf16[1024,512]{1,0:T(8,128)(2,1)}, u32[]{:S(2)}) copy-start(bf16[1024,512]{1,0:T(8,128)(2,1)} %param.29) | copy-start | bytes 3145732
  7.2 24.9 %copy-start.4 = (bf16[512,512]{1,0:T(8,128)(2,1)S(1)}, bf16[512,512]{1,0:T(8,128)(2,1)}, u32[]{:S(2)}) copy-start(bf16[512,512]{1,0:T(8,128)(2,1)} %param.19) | copy-start | bytes 1572868
  7.2 24.3 %copy-start.39 = (s32[512]{0:T(512)S(1)}, s32[512]{0:T(512)}, u32[]{:S(2)}) copy-start(s32[512]{0:T(512)} %param.24) | copy-start | bytes 6148
  9.9 31.1 %collective-permute-start = (bf16[32,512]{1,0:T(8,128)(2,1)S(1)}, bf16[32,512]{1,0:T(8,128)(2,1)S(1)}, u32[]{:S(2)}, u32[]{:S(2)}) collective-permute-start(bf16[32,512]{1,0:T(8,128)(2,1)S(1)} %broadcast_select_fusion.4), channel_id=1, source_target_pairs={{0,16},{16,32},{32,48},{48,64},{64,80},{80,96},{96,112},{1,17},{17... | collective-permute-start | bytes 98312 | tf_op jit(solution)/shard_map/ppermute | solution.py:11
  16.7 24.4 %collective-permute-start.1 = (bf16[32,512]{1,0:T(8,128)(2,1)S(1)}, bf16[32,512]{1,0:T(8,128)(2,1)S(1)}, u32[]{:S(2)}, u32[]{:S(2)}) collective-permute-start(bf16[32,512]{1,0:T(8,128)(2,1)S(1)} %broadcast_select_fusion.3), channel_id=1, source_target_pairs={{16,0},{32,16},{48,32},{64,48},{80,64},{96,80},{112,96},{17,1},{33... | collective-permute-start | bytes 98312 | tf_op jit(solution)/shard_map/ppermute | solution.py:11
  20.4 20.6 %collective-permute-start.2 = (bf16[32,512]{1,0:T(8,128)(2,1)S(1)}, bf16[32,512]{1,0:T(8,128)(2,1)S(1)}, u32[]{:S(2)}, u32[]{:S(2)}) collective-permute-start(bf16[32,512]{1,0:T(8,128)(2,1)S(1)} %broadcast_select_fusion.2), channel_id=1, source_target_pairs={{0,1},{1,2},{2,3},{3,4},{4,5},{5,6},{6,7},{7,8},{8,9},{9,10},{10,1... | collective-permute-start | bytes 98312 | tf_op jit(solution)/shard_map/ppermute | solution.py:11
  25.5 15.6 %collective-permute-start.3 = (bf16[32,512]{1,0:T(8,128)(2,1)S(1)}, bf16[32,512]{1,0:T(8,128)(2,1)S(1)}, u32[]{:S(2)}, u32[]{:S(2)}) collective-permute-start(bf16[32,512]{1,0:T(8,128)(2,1)S(1)} %broadcast_select_fusion.1), channel_id=1, source_target_pairs={{1,0},{2,1},{3,2},{4,3},{5,4},{6,5},{7,6},{8,7},{9,8},{10,9},{11,1... | collective-permute-start | bytes 98312 | tf_op jit(solution)/shard_map/ppermute | solution.py:11
  51.6 5.6 %copy-start.19 = (bf16[512,512]{1,0:T(8,128)(2,1)S(1)}, bf16[512,512]{1,0:T(8,128)(2,1)}, u32[]{:S(2)}) copy-start(bf16[512,512]{1,0:T(8,128)(2,1)} %param.28) | copy-start | bytes 1572868
  76.2 20.1 %copy-start.30 = (s32[1,1024]{1,0:T(1,128)S(1)}, s32[1,1024]{1,0:T(1,128)}, u32[]{:S(2)}) copy-start(s32[1,1024]{1,0:T(1,128)} %param.25) | copy-start | bytes 12292
  80.8 30.4 %all-to-all-start = ((bf16[128,8,512]{2,1,0:T(8,128)(2,1)}), bf16[128,8,512]{2,1,0:T(8,128)(2,1)S(1)}, u32[]{:S(2)}, u32[]{:S(2)}) async-start(bf16[128,8,512]{2,1,0:T(8,128)(2,1)} %bitcast.5), calls=%async_computation | async-start | bytes 2097152 | tf_op jit(solution)/shard_map/all_to_all | solution.py:45
  111.2 24.4 %all-to-all-start.2 = ((bf16[128,8,512]{2,1,0:T(8,128)(2,1)}), bf16[128,8,512]{2,1,0:T(8,128)(2,1)}, u32[]{:S(2)}, u32[]{:S(2)}) async-start(bf16[128,8,512]{2,1,0:T(8,128)(2,1)} %bitcast.9), calls=%async_computation.2 | async-start | bytes 2097152 | tf_op jit(solution)/shard_map/all_to_all | solution.py:45
  117.0 18.6 %copy-start.41 = (f32[128]{0:T(128)}, f32[128]{0:T(128)S(1)}, u32[]{:S(2)}) copy-start(f32[128]{0:T(128)S(1)} %broadcast_maximum_fusion) | copy-start | bytes 1540
  117.9 19.2 %copy-start.28 = (bf16[128,512]{1,0:T(8,128)(2,1)}, bf16[128,512]{1,0:T(8,128)(2,1)S(1)}, u32[]{:S(2)}) copy-start(bf16[128,512]{1,0:T(8,128)(2,1)S(1)} %fusion.7) | copy-start | bytes 393220
  143.1 5.1 %copy-start.37 = (pred[1024]{0:T(1024)(128)(4,1)S(1)}, pred[1024]{0:T(1024)(128)(4,1)}, u32[]{:S(2)}) copy-start(pred[1024]{0:T(1024)(128)(4,1)} %get-tuple-element.37) | copy-start | bytes 3076
  143.1 5.1 %copy-start.38 = (pred[1024]{0:T(1024)(128)(4,1)S(1)}, pred[1024]{0:T(1024)(128)(4,1)}, u32[]{:S(2)}) copy-start(pred[1024]{0:T(1024)(128)(4,1)} %get-tuple-element.38) | copy-start | bytes 3076
  148.2 7.8 %copy-start.34 = (s32[512]{0:T(512)S(1)}, s32[512]{0:T(512)}, u32[]{:S(2)}) copy-start(s32[512]{0:T(512)} %get-tuple-element.24) | copy-start | bytes 6148
  151.1 26.4 %copy-start.35 = (pred[512]{0:T(512)(128)(4,1)S(1)}, pred[512]{0:T(512)(128)(4,1)}, u32[]{:S(2)}) copy-start(pred[512]{0:T(512)(128)(4,1)} %get-tuple-element.23) | copy-start | bytes 1540
  151.1 23.8 %all-to-all-start.3 = ((bf16[128,8,512]{2,1,0:T(8,128)(2,1)}), bf16[128,8,512]{2,1,0:T(8,128)(2,1)S(1)}, u32[]{:S(2)}, u32[]{:S(2)}) async-start(bf16[128,8,512]{2,1,0:T(8,128)(2,1)} %get-tuple-element.39), calls=%async_computation.3 | async-start | bytes 2097152 | tf_op jit(solution)/shard_map/all_to_all | solution.py:45
  155.9 175.0 %all-reduce.7.cloned.1.call-start = ((), (), s32[]{:S(2)}) async-start(), calls=%async_computation.5 | async-start | bytes 14680064 | tf_op jit(solution)/shard_map/psum | solution.py:152
  182.1 9.2 %copy-start.31 = (pred[2048]{0:T(1024)(128)(4,1)S(1)}, pred[2048]{0:T(1024)(128)(4,1)}, u32[]{:S(2)}) copy-start(pred[2048]{0:T(1024)(128)(4,1)} %get-tuple-element.53) | copy-start | bytes 6148
  182.1 14.4 %copy-start.20 = (bf16[512,512]{1,0:T(8,128)(2,1)S(1)}, bf16[512,512]{1,0:T(8,128)(2,1)}, u32[]{:S(2)}) copy-start(bf16[512,512]{1,0:T(8,128)(2,1)} %param.28) | copy-start | bytes 1572868
  191.3 5.1 %copy-start.2 = (f32[2048,512]{1,0:T(8,128)S(1)}, f32[2048,512]{1,0:T(8,128)}, u32[]{:S(2)}) copy-start(f32[2048,512]{1,0:T(8,128)} %gather_fusion.1) | copy-start | bytes 12582916
  191.3 6.1 %copy-start.3 = (f32[2048,512]{1,0:T(8,128)S(1)}, f32[2048,512]{1,0:T(8,128)}, u32[]{:S(2)}) copy-start(f32[2048,512]{1,0:T(8,128)} %gather_fusion) | copy-start | bytes 12582916
  191.3 6.1 %copy-start.32 = (pred[2048]{0:T(1024)(128)(4,1)S(1)}, pred[2048]{0:T(1024)(128)(4,1)}, u32[]{:S(2)}) copy-start(pred[2048]{0:T(1024)(128)(4,1)} %get-tuple-element.54) | copy-start | bytes 6148
  229.0 10.3 %copy-start.6 = (f32[512,512]{1,0:T(8,128)}, f32[512,512]{1,0:T(8,128)S(1)}, u32[]{:S(2)}) copy-start(f32[512,512]{1,0:T(8,128)S(1)} %scatter_custom_fusion.3) | copy-start | bytes 3145732
  229.0 4.9 %copy-start.23 = (bf16[512,512]{1,0:T(8,128)(2,1)S(1)}, bf16[512,512]{1,0:T(8,128)(2,1)}, u32[]{:S(2)}) copy-start(bf16[512,512]{1,0:T(8,128)(2,1)} %copy-done.22) | copy-start | bytes 1572868
  229.0 4.9 %copy-start.25 = (bf16[512,512]{1,0:T(8,128)(2,1)S(1)}, bf16[512,512]{1,0:T(8,128)(2,1)}, u32[]{:S(2)}) copy-start(bf16[512,512]{1,0:T(8,128)(2,1)} %copy-done.24) | copy-start | bytes 1572868
  229.0 7.0 %copy-start.11 = (bf16[512,512]{1,0:T(8,128)(2,1)S(1)}, bf16[512,512]{1,0:T(8,128)(2,1)}, u32[]{:S(2)}) copy-start(bf16[512,512]{1,0:T(8,128)(2,1)} %gather_fusion.10) | copy-start | bytes 1572868
  229.0 7.0 %copy-start.21 = (bf16[512,512]{1,0:T(8,128)(2,1)S(1)}, bf16[512,512]{1,0:T(8,128)(2,1)}, u32[]{:S(2)}) copy-start(bf16[512,512]{1,0:T(8,128)(2,1)} %param.20) | copy-start | bytes 1572868
  229.0 7.0 %copy-start.36 = (pred[512]{0:T(512)(128)(4,1)S(1)}, pred[512]{0:T(512)(128)(4,1)}, u32[]{:S(2)}) copy-start(pred[512]{0:T(512)(128)(4,1)} %get-tuple-element.23) | copy-start | bytes 1540
  229.0 7.0 %copy-start.43 = (f32[512,512]{1,0:T(8,128)S(1)}, f32[512,512]{1,0:T(8,128)}, u32[]{:S(2)}) copy-start(f32[512,512]{1,0:T(8,128)} %copy-done.42) | copy-start | bytes 3145732
  240.7 234.1 %all-reduce.5.cloned.1.call-start = ((), (), s32[]{:S(2)}) async-start(), calls=%async_computation.4 | async-start | bytes 14680064 | tf_op jit(solution)/shard_map/psum | solution.py:151
  330.9 8.4 %copy-start.33 = (s32[1,4,32]{2,1,0:T(4,128)S(1)}, s32[1,4,32]{2,1,0:T(4,128)}, u32[]{:S(2)}) copy-start(s32[1,4,32]{2,1,0:T(4,128)} %param.23) | copy-start | bytes 1540
  330.9 35.0 %all-to-all-start.1 = ((bf16[128,8,512]{2,1,0:T(8,128)(2,1)}), bf16[128,8,512]{2,1,0:T(8,128)(2,1)S(1)}, u32[]{:S(2)}, u32[]{:S(2)}) async-start(bf16[128,8,512]{2,1,0:T(8,128)(2,1)} %get-tuple-element.40), calls=%async_computation.1 | async-start | bytes 2097152 | tf_op jit(solution)/shard_map/all_to_all | solution.py:45
  365.9 13.2 %copy-start.12 = (bf16[512,512]{1,0:T(8,128)(2,1)S(1)}, bf16[512,512]{1,0:T(8,128)(2,1)}, u32[]{:S(2)}) copy-start(bf16[512,512]{1,0:T(8,128)(2,1)} %gather_fusion.10) | copy-start | bytes 1572868
  367.9 11.2 %copy-start.7 = (f32[512,512]{1,0:T(8,128)S(1)}, f32[512,512]{1,0:T(8,128)}, u32[]{:S(2)}) copy-start(f32[512,512]{1,0:T(8,128)} %copy-done.6) | copy-start | bytes 3145732
  367.9 11.2 %copy-start.9 = (f32[512,1024]{1,0:T(8,128)S(1)}, f32[512,1024]{1,0:T(8,128)}, u32[]{:S(2)}) copy-start(f32[512,1024]{1,0:T(8,128)} %copy-done.8) | copy-start | bytes 6291460
  367.9 11.2 %copy-start.14 = (bf16[512,512]{1,0:T(8,128)(2,1)S(1)}, bf16[512,512]{1,0:T(8,128)(2,1)}, u32[]{:S(2)}) copy-start(bf16[512,512]{1,0:T(8,128)(2,1)} %param.27) | copy-start | bytes 1572868
  367.9 12.9 %copy-start.27 = (bf16[512,512]{1,0:T(8,128)(2,1)S(1)}, bf16[512,512]{1,0:T(8,128)(2,1)}, u32[]{:S(2)}) copy-start(bf16[512,512]{1,0:T(8,128)(2,1)} %copy-done.26) | copy-start | bytes 1572868
  369.7 12.1 %collective-permute-start.7 = (bf16[32,512]{1,0:T(8,128)(2,1)S(1)}, bf16[32,512]{1,0:T(8,128)(2,1)S(1)}, u32[]{:S(2)}, u32[]{:S(2)}) collective-permute-start(bf16[32,512]{1,0:T(8,128)(2,1)S(1)} %get-tuple-element.34), channel_id=1, source_target_pairs={{0,1},{1,2},{2,3},{3,4},{4,5},{5,6},{6,7},{7,8},{8,9},{9,10},{10,1... | collective-permute-start | bytes 98312 | tf_op jit(solution)/shard_map/ppermute | solution.py:11
  372.0 9.8 %collective-permute-start.6 = (bf16[32,512]{1,0:T(8,128)(2,1)S(1)}, bf16[32,512]{1,0:T(8,128)(2,1)S(1)}, u32[]{:S(2)}, u32[]{:S(2)}) collective-permute-start(bf16[32,512]{1,0:T(8,128)(2,1)S(1)} %get-tuple-element.35), channel_id=1, source_target_pairs={{1,0},{2,1},{3,2},{4,3},{5,4},{6,5},{7,6},{8,7},{9,8},{10,9},{11,1... | collective-permute-start | bytes 98312 | tf_op jit(solution)/shard_map/ppermute | solution.py:11
  373.3 8.5 %collective-permute-start.5 = (bf16[32,512]{1,0:T(8,128)(2,1)S(1)}, bf16[32,512]{1,0:T(8,128)(2,1)S(1)}, u32[]{:S(2)}, u32[]{:S(2)}) collective-permute-start(bf16[32,512]{1,0:T(8,128)(2,1)S(1)} %get-tuple-element.36), channel_id=1, source_target_pairs={{0,16},{16,32},{32,48},{48,64},{64,80},{80,96},{96,112},{1,17},{17... | collective-permute-start | bytes 98312 | tf_op jit(solution)/shard_map/ppermute | solution.py:11
  377.1 5.6 %collective-permute-start.4 = (bf16[32,512]{1,0:T(8,128)(2,1)S(1)}, bf16[32,512]{1,0:T(8,128)(2,1)S(1)}, u32[]{:S(2)}, u32[]{:S(2)}) collective-permute-start(bf16[32,512]{1,0:T(8,128)(2,1)S(1)} %get-tuple-element.33), channel_id=1, source_target_pairs={{16,0},{32,16},{48,32},{64,48},{80,64},{96,80},{112,96},{17,1},{33... | collective-permute-start | bytes 98312 | tf_op jit(solution)/shard_map/ppermute | solution.py:11
  384.5 97.8 %copy-start.18 = (f32[512,512]{1,0:T(8,128)}, f32[512,512]{1,0:T(8,128)S(1)}, u32[]{:S(2)}) copy-start(f32[512,512]{1,0:T(8,128)S(1)} %scatter_custom_fusion.5) | copy-start | bytes 3145732
  474.8 4.8 copy-start.17
  474.8 5.9 %copy-start.13 = (f32[1024,512]{1,0:T(8,128)S(1)}, f32[1024,512]{1,0:T(8,128)}, u32[]{:S(2)}) copy-start(f32[1024,512]{1,0:T(8,128)} %get-tuple-element.14) | copy-start | bytes 6291460
  477.3 5.0 %copy-start.16 = (f32[512,512]{1,0:T(8,128)S(1)}, f32[512,512]{1,0:T(8,128)}, u32[]{:S(2)}) copy-start(f32[512,512]{1,0:T(8,128)} %get-tuple-element.15) | copy-start | bytes 3145732
  480.7 3.7 copy-start.1
  (10 other events, 16.3 us)
Sparse Core Ops, SparseCore 0:
  240.8 90.0 all-reduce.6
  335.1 139.7 all-reduce.4
